TPU v7x, 32 devices: a whole 2x2x4 slice. The times are simulated.
32 devices in a mesh: lines: 2 (over y), shots: 16 (over z, x, core).
Axes of the slice: x: 2, y: 2, z: 4, core: 2. Of those that a mesh axis runs over, the one named last changes fastest.
Arguments:
- records: bfloat16 [2048, 1024, 256], P(('lines', 'shots')), parts along dimension 0, may hold values from -6 to 6
- missing: int32 [256], P('lines'), parts along dimension 0, may hold values from 0 to 1023, as said below
- neighbours: int32 [256, 3], P('lines'), parts along dimension 0, may hold values from 0 to 1023, as said below
- weights: float32 [256, 3], P('lines'), parts along dimension 0, may hold values from 0.2 to 0.6
- freq_bins: int32 [8], replicated, may hold values from 1 to 127, as said below
Outputs:
- multiples: bfloat16 [2048, 1024, 256], P(('lines', 'shots')), parts along dimension 0
There are 2 independent parts, one for each index of `lines`. A program takes and returns all parts, laid end to end along the dimension named above; an argument that names none is the same for every part. Nothing has to cross between parts.
Inputs may be any that keep to these rules, and one draw needn't show every extreme that they name: `missing`: distinct and ascending; any two missing shots lie 3 or more apart, and every shot within 2 of a missing shot is recorded. `neighbours`: row i names 3 distinct recorded shots, each within 2 of missing[i]. `freq_bins`: 8 distinct bins.
All inputs are finite; a program needn't handle non-finite values.
Results may differ from a plain program's by a relative error of at most 0.0079.
Values may be sent and summed in bfloat16 or wider, within the bound.
No kernel may reach another device: no remote copies, remote signals or barrier semaphores. Data moves between devices by JAX's collectives and lax.ppermute only.
A program may use at most 192 MiB of HBM per device.

v0:
```python
import math
import jax
import jax.numpy as jnp
from jax import lax
from jax.sharding import PartitionSpec as P


def from_partner(array, axis, stride):
    return lax.ppermute(array, axis, [(i, i ^ 1 << stride) for i in range(lax.axis_size(axis))])


def tables(freq_bins, sample_count):
    bin_count = freq_bins.shape[0]
    sample_ids = jnp.arange(sample_count, dtype=jnp.int32)
    phases = freq_bins[None, :] * sample_ids[:, None] % sample_count
    angles = phases.astype(jnp.float32) * (2.0 * math.pi / sample_count)
    trig_pair = jnp.stack([jnp.cos(angles), -jnp.sin(angles)], axis=-1)
    forward = (trig_pair / math.sqrt(sample_count)).astype(jnp.bfloat16)
    inverse = (trig_pair * math.sqrt(2.0 / bin_count)).astype(jnp.bfloat16)
    return (forward, inverse)


def add_block(summed, right_source, block_piece, source_part, width):
    right_rows = lax.dynamic_slice_in_dim(right_source, source_part * width, width, 2)
    right_real = right_rows[:, 0]
    right_imag = right_rows[:, 1]
    left_side = jnp.concatenate([block_piece[:, 0], block_piece[:, 1]], axis=-1)
    right_side = jnp.concatenate(
        [
            jnp.concatenate([right_real, right_imag], axis=-1),
            jnp.concatenate([-right_imag, right_real], axis=-1),
        ],
        axis=1,
    )
    return summed + jnp.einsum(
        "zsk,zkc->zsc", left_side, right_side, preferred_element_type=jnp.float32
    )


def shards(records, missing, neighbours, weights, freq_bins):
    devices = lax.axis_size("shots")
    position = lax.axis_index("shots")
    shot_rows = records.shape[0]
    matrix_order = records.shape[1]
    sample_count = records.shape[2]
    half = matrix_order // 2
    couples = devices // 2
    neigh_count = neighbours.shape[1]
    forward, inverse = tables(freq_bins, sample_count)
    blocked = records.reshape(shot_rows, 2, half, sample_count)
    spectra = jnp.einsum(
        "shrt,tpc->phcsr", blocked, forward, preferred_element_type=jnp.float32
    ).astype(jnp.bfloat16)
    outgoing = spectra.reshape(devices, 2, shot_rows, half)
    incoming = lax.all_to_all(outgoing, "shots", split_axis=0, concat_axis=2, tiled=True)
    own_block = incoming
    filled_rows = jnp.zeros(
        own_block.shape[:2] + (missing.shape[0], own_block.shape[3]), jnp.float32
    )
    for slot_index in range(neigh_count):
        picked = jnp.take(own_block, neighbours[:, slot_index], axis=2)
        filled_rows = filled_rows + weights[:, slot_index][:, None] * picked.astype(jnp.float32)
    own_block = own_block.at[:, :, missing, :].set(filled_rows.astype(jnp.bfloat16))
    factor = -1.0 / math.sqrt(matrix_order)
    member = position % 2
    other_half = from_partner(own_block, "shots", 0)
    summed = jnp.zeros((1, matrix_order, 2 * half), jnp.float32)
    summed = add_block(summed, own_block, own_block, member, half)
    summed = add_block(summed, own_block, other_half, 1 - member, half)
    predicted = (summed * factor).astype(jnp.bfloat16)
    outgoing_back = predicted.reshape(1, 1, matrix_order, 2, half)
    returned = lax.all_to_all(outgoing_back, "shots", split_axis=2, concat_axis=0, tiled=True)
    returned = returned.reshape(couples, 2, shot_rows, 2, half)
    inverse_pair = jnp.transpose(inverse, (1, 2, 0))
    multiples = jnp.einsum(
        "phsir,pit->shrt", returned, inverse_pair, preferred_element_type=jnp.float32
    )
    return multiples.astype(jnp.bfloat16).reshape(shot_rows, matrix_order, sample_count)


def solution(mesh):
    return jax.shard_map(
        shards,
        mesh=mesh,
        in_specs=(
            P(("lines", "shots"), None, None),
            P("lines"),
            P("lines", None),
            P("lines", None),
            P(),
        ),
        out_specs=P(("lines", "shots"), None, None),
        check_vma=False,
    )
```

profile of v0, /device:TPU:1, one launch (start us, length us, event | category | flops | bytes accessed | tf_op | source)
XLA Modules:
  0.0 226.2 jit_solution(15952306101126947677)
XLA Ops:
  0.0 0.8 fusion.33
  0.8 14.2 %convert_bitcast_fusion = bf16[8,2,2,64,512]{4,0,1,3,2:T(8,128)(2,1)S(1)} fusion(bf16[64,2,512,256,1]{3,2,1,0,4:T(8,128)(2,1)} %bitcast.127, f32[256,8,1]{0,1,2:T(8,128)S(1)} %get-tuple-element.30, f32[256,8,1]{0,1,2:T(8,128)S(1)} %get-tuple-element.29), kind=kOutput, calls=%fused_computation.31 | convolution fusion | flops 537931776 | bytes 35667968 | tf_op jit(solution)/shard_map/shrt,tpc->phcsr/dot_general | solution.py:51
  15.0 2.5 %copy.40 = bf16[8,2,2,64,512]{4,3,2,1,0:T(8,128)(2,1)} copy(bf16[8,2,2,64,512]{4,0,1,3,2:T(8,128)(2,1)S(1)} %convert_bitcast_fusion) | data formatting | bytes 4194304 | tf_op jit(solution)/shard_map/convert_element_type | solution.py:53
  17.5 7.4 %all-to-all-start = ((bf16[16,2,64,512]{3,2,1,0:T(8,128)(2,1)}), bf16[16,2,64,512]{3,2,1,0:T(8,128)(2,1)S(1)}, u32[]{:S(2)}, u32[]{:S(2)}) async-start(bf16[16,2,64,512]{3,2,1,0:T(8,128)(2,1)} %bitcast.131), calls=%async_computation | async-start | bytes 4194304 | tf_op jit(solution)/shard_map/all_to_all | solution.py:55
  25.0 41.4 %all-to-all-done = bf16[16,2,64,512]{3,2,1,0:T(8,128)(2,1)S(1)} async-done(((bf16[16,2,64,512]{3,2,1,0:T(8,128)(2,1)}), bf16[16,2,64,512]{3,2,1,0:T(8,128)(2,1)S(1)}, u32[]{:S(2)}, u32[]{:S(2)}) %all-to-all-start) | async-done | bytes 2097184 | tf_op jit(solution)/shard_map/all_to_all | solution.py:55
  66.4 1.3 copy-done
  67.8 3.9 %copy.41 = bf16[1,2,16,64,512]{4,1,3,2,0:T(2,128)(2,1)S(1)} copy(bf16[1,2,16,64,512]{4,3,1,2,0:T(8,128)(2,1)} %bitcast.128) | data formatting | bytes 4194304 | tf_op jit(solution)/shard_map/all_to_all | solution.py:55
  71.9 3.5 %copy.77 = bf16[1,2,1024,512]{3,1,2,0:T(2,128)(2,1)} copy(bf16[1,2,1024,512]{3,2,1,0:T(8,128)(2,1)S(1)} %bitcast.132) | data formatting | bytes 4194304 | tf_op jit(solution)/shard_map/all_to_all | solution.py:55
  75.4 2.7 %gather_fusion.2 = bf16[128,2,512]{2,1,0:T(2,128)(2,1)S(1)} fusion(bf16[2,1024,512]{2,0,1:T(2,128)(2,1)} %bitcast.137, s32[1024]{0:T(1024)S(1)} %get-tuple-element.31), kind=kCustom, calls=%fused_computation.2.clone | custom fusion | bytes 524800 | tf_op jit(solution)/shard_map/jit(_take)/gather | solution.py:61
  78.1 2.7 %gather_fusion.1 = bf16[128,2,512]{2,1,0:T(2,128)(2,1)S(1)} fusion(bf16[2,1024,512]{2,0,1:T(2,128)(2,1)} %bitcast.138, s32[1024]{0:T(1024)S(1)} %get-tuple-element.32), kind=kCustom, calls=%fused_computation.1.clone | custom fusion | bytes 524800 | tf_op jit(solution)/shard_map/jit(_take)/gather | solution.py:61
  80.8 2.7 %gather_fusion = bf16[128,2,512]{2,1,0:T(2,128)(2,1)S(1)} fusion(bf16[2,1024,512]{2,0,1:T(2,128)(2,1)} %bitcast.139, s32[1024]{0:T(1024)S(1)} %pad_clamp_fusion.2), kind=kCustom, calls=%fused_computation.clone | custom fusion | bytes 524800 | tf_op jit(solution)/shard_map/jit(_take)/gather | solution.py:61
  84.1 4.4 %scatter_fusion = bf16[2,1024,512]{2,0,1:T(2,128)(2,1)S(1)} fusion(bf16[2,1024,512]{2,0,1:T(2,128)(2,1)S(1)} %bitcast.124, s32[128]{0:T(128)S(1)} %compare_select_fusion.3, bf16[128,2,512]{2,1,0:T(2,128)(2,1)S(1)} %copy.49), kind=kCustom, calls=%fused_computation.3 | custom fusion | bytes 786944 | tf_op jit(solution)/shard_map/scatter | solution.py:63
  88.5 1.4 constant_dynamic-slice_fusion
  90.4 3.2 %fusion.43 = (bf16[1,1,1024,512]{3,1,2,0:T(2,128)(2,1)S(1)}, bf16[1,1,1024,512]{3,1,2,0:T(2,128)(2,1)S(1)}) fusion(bf16[1,2,1024,512]{3,1,2,0:T(2,128)(2,1)S(1)} %bitcast.126), kind=kLoop, calls=%fused_computation.89 | loop fusion | bytes 4194304 | tf_op jit(solution)/shard_map/slice | solution.py:27
  93.6 0.3 copy.81
  93.9 0.3 copy.80
  94.5 2.5 %fusion.1 = f32[1024,1024]{0,1:T(8,128)S(1)} fusion(bf16[1,1024,512]{2,1,0:T(8,128)(2,1)S(1)} %bitcast.142, bf16[1,1024,512]{2,1,0:T(8,128)(2,1)S(1)} %bitcast.141, bf16[1,512,512]{2,1,0:T(8,128)(2,1)S(1)} %get-tuple-element.21, bf16[1,512,512]{2,1,0:T(8,128)(2,1)S(1)} %fusion.40, bf16[1,512,512]{2,1,0:T(8,128)(2,1)S(1)} %get-tuple-element.20), kind=kOutput, calls=%fused_computation.8 | convolution fusion | flops 2160066560 | bytes 7864320 | tf_op jit(solution)/shard_map/zsk,zkc->zsc/dot_general | solution.py:35
  96.9 3.0 %fusion.42 = (bf16[1,1,1024,512]{3,1,2,0:T(2,128)(2,1)S(1)}, bf16[1,1,1024,512]{3,1,2,0:T(2,128)(2,1)S(1)}) fusion(bf16[1,2,1024,512]{3,1,2,0:T(2,128)(2,1)S(1)} %collective-permute-done), kind=kLoop, calls=%fused_computation.88 | loop fusion | bytes 4194304 | tf_op jit(solution)/shard_map/slice | solution.py:27
  99.9 0.3 copy.79
  100.5 4.0 %multiply_convert_fusion = bf16[1024,1024]{0,1:T(8,128)(2,1)} fusion(f32[1024,1024]{0,1:T(8,128)S(1)} %fusion.1, bf16[1,512,512]{2,1,0:T(8,128)(2,1)S(1)} %get-tuple-element.19, bf16[1,512,512]{2,1,0:T(8,128)(2,1)S(1)} %fusion.41, bf16[1,512,512]{2,1,0:T(8,128)(2,1)S(1)} %get-tuple-element.18, bf16[1,1024,512]{2,1,0:T(8,128)(2,1)S(1)} %bitcast.144, ...), kind=kOutput, calls=%fused_computation.6 | convolution fusion | flops 2163212288 | bytes 9961472 | tf_op jit(solution)/shard_map/zsk,zkc->zsc/dot_general | solution.py:35
  104.5 4.8 %copy.52 = bf16[1,1,1024,2,512]{4,3,1,0,2:T(2,128)(2,1)S(1)} copy(bf16[1,1,1024,2,512]{2,4,3,1,0:T(8,128)(2,1)} %bitcast.140) | data formatting | bytes 4194304 | tf_op jit(solution)/shard_map/reshape | solution.py:71
  109.3 58.5 %all_to_all.27 = bf16[1,1,1024,2,512]{4,3,1,0,2:T(2,128)(2,1)S(1)} all-to-all(bf16[1,1,1024,2,512]{4,3,1,0,2:T(2,128)(2,1)S(1)} %copy.52), channel_id=1, replica_groups=mesh['lines'=2,'shots'=16] {'shots'}, dimensions={2} | all-to-all | bytes 4194304 | tf_op jit(solution)/shard_map/all_to_all | solution.py:72
  167.8 14.1 %fusion = bf16[64,2,512,256]{2,3,0,1:T(8,128)(2,1)} fusion(bf16[8,2,64,2,512]{4,3,2,1,0:T(2,128)(2,1)S(1)} %bitcast.130, f32[256,8,1]{0,1,2:T(8,128)S(1)} %get-tuple-element.30, f32[256,8,1]{0,1,2:T(8,128)S(1)} %get-tuple-element.29), kind=kOutput, calls=%fused_computation.5 | convolution fusion | flops 553660416 | bytes 35667968 | tf_op jit(solution)/shard_map/phsir,pit->shrt/dot_general | solution.py:75
  181.9 44.2 %copy.55 = bf16[64,2,512,256]{3,2,1,0:T(8,128)(2,1)} copy(bf16[64,2,512,256]{2,3,0,1:T(8,128)(2,1)} %fusion) | data formatting | bytes 67108864 | tf_op jit(solution)/shard_map/convert_element_type | solution.py:78
  (26 shorter events, 1.7 us)
Async XLA Ops:
  17.5 7.5 %copy-start.3 = (s32[128,3]{0,1:T(4,128)S(1)}, s32[128,3]{0,1:T(4,128)}, u32[]{:S(2)}) copy-start(s32[128,3]{0,1:T(4,128)} %param.9) | copy-start | bytes 4612
  17.5 7.5 %copy-start.4 = (s32[128]{0:T(128)S(1)}, s32[128]{0:T(128)}, u32[]{:S(2)}) copy-start(s32[128]{0:T(128)} %param.8) | copy-start | bytes 1540
  17.5 7.5 %copy-start.2 = (f32[128,3]{0,1:T(4,128)S(1)}, f32[128,3]{0,1:T(4,128)}, u32[]{:S(2)}) copy-start(f32[128,3]{0,1:T(4,128)} %param.10) | copy-start | bytes 4612
  17.5 49.0 %all-to-all-start = ((bf16[16,2,64,512]{3,2,1,0:T(8,128)(2,1)}), bf16[16,2,64,512]{3,2,1,0:T(8,128)(2,1)S(1)}, u32[]{:S(2)}, u32[]{:S(2)}) async-start(bf16[16,2,64,512]{3,2,1,0:T(8,128)(2,1)} %bitcast.131), calls=%async_computation | async-start | bytes 4194304 | tf_op jit(solution)/shard_map/all_to_all | solution.py:55
  66.4 1.3 copy-start
  67.8 3.9 %copy-start.1 = (bf16[16,2,64,512]{3,2,1,0:T(8,128)(2,1)S(1)}, bf16[16,2,64,512]{3,2,1,0:T(8,128)(2,1)}, u32[]{:S(2)}) copy-start(bf16[16,2,64,512]{3,2,1,0:T(8,128)(2,1)} %copy-done) | copy-start | bytes 6291460
  90.3 6.6 %collective-permute-start = (bf16[1,2,1024,512]{3,1,2,0:T(2,128)(2,1)S(1)}, bf16[1,2,1024,512]{3,1,2,0:T(2,128)(2,1)S(1)}, u32[]{:S(2)}, u32[]{:S(2)}) collective-permute-start(bf16[1,2,1024,512]{3,1,2,0:T(2,128)(2,1)S(1)} %bitcast.125), channel_id=1, source_target_pairs={{0,1},{1,0},{2,3},{3,2},{4,5},{5,4},{6,7},{7,6},{8,9},{9,8},{10,11... | collective-permute-start | bytes 6291464 | tf_op jit(solution)/shard_map/ppermute | solution.py:9
where the time goes:
time: 228 us; the launch traced here: 226 us
  local copies, waits for them, and re-layouts  82.5 us (36%)
  blocking collectives  58.5 us (26%)
  waiting for transfers between devices  41.4 us (18%)
  matrix products  34.7 us (15%)
  starting transfers between devices  7.51 us (3%)
    all_to_all x1, blocking collectives, shards(): lax.all_to_all(outgoing_back, 'shots', split_axis=2, concat_axis=0, tiled...  58.5 us
    convert_element_type x1, local copies, waits for them, and re-layouts, shards(): multiples.astype(jnp.bfloat16)  44.2 us
    all_to_all x1, waiting for transfers between devices, shards(): lax.all_to_all(outgoing, 'shots', split_axis=0, concat_axis=2, tiled=True)  41.4 us
    dot_general x1, matrix products, shards(): jnp.einsum('shrt,tpc->phcsr', blocked, forward, preferred_element_type=jn...  14.2 us
    dot_general x1, matrix products, shards(): jnp.einsum('phsir,pit->shrt', returned, inverse_pair, preferred_element_t...  14.1 us
    gather x3, local copies, waits for them, and re-layouts, shards(): picked = jnp.take(own_block, neighbours[:, slot_index], axis=2)  8.18 us
    all_to_all x3, local copies, waits for them, and re-layouts, shards(): lax.all_to_all(outgoing, 'shots', split_axis=0, concat_axis=2, tiled=True)  7.59 us
    all_to_all x1, starting transfers between devices, shards(): lax.all_to_all(outgoing, 'shots', split_axis=0, concat_axis=2, tiled=True)  7.44 us
  transfers between devices with their start and end apart: 2, of which 1 were waited for; matrix products, arithmetic and copies ran while one was open for 3% of the time, Pallas kernels for 0%

commit v1 on v0

--- a/solution.py
+++ b/solution.py
@@ -1,8 +1,18 @@
+import functools
 import math
 import jax
 import jax.numpy as jnp
 from jax import lax
 from jax.sharding import PartitionSpec as P
+
+
+def lay_group_up(z, peer_axis):
+    return jnp.concatenate(
+        lax.all_to_all(jnp.stack(jnp.split(z, lax.psum(1, peer_axis), 0)), peer_axis, 0, 0), 2
+    )
+
+
+_keep_up_edges = functools.partial(lay_group_up, peer_axis="shots")
 
 
 def from_partner(array, axis, stride):
@@ -52,7 +62,7 @@
         "shrt,tpc->phcsr", blocked, forward, preferred_element_type=jnp.float32
     ).astype(jnp.bfloat16)
     outgoing = spectra.reshape(devices, 2, shot_rows, half)
-    incoming = lax.all_to_all(outgoing, "shots", split_axis=0, concat_axis=2, tiled=True)
+    incoming = _keep_up_edges(outgoing)
     own_block = incoming
     filled_rows = jnp.zeros(
         own_block.shape[:2] + (missing.shape[0], own_block.shape[3]), jnp.float32

time: 228 us -> 237 us (1.039)
  local copies, waits for them, and re-layouts: 82.5 us -> 91.8 us
    unnamed x17 -> x32, local copies, waits for them, and re-layouts: 4.25 us -> 14.2 us
    all_to_all x3 -> x0, local copies, waits for them, and re-layouts: 7.59 us -> none  [shards(): lax.all_to_all(outgoing, 'shots', split_axis=0, concat_axis=2, tiled=True)]
    reshape x0 -> x3, local copies, waits for them, and re-layouts: none -> 7.59 us  [lay_group_up(): jnp.concatenate(lax.all_to_all(jnp.stack(jnp.split(z, lax.psum(1, peer_ax...]
where the time goes in v1:
time: 237 us; the launch traced here: 235 us
  local copies, waits for them, and re-layouts  91.8 us (39%)
  blocking collectives  58.5 us (25%)
  waiting for transfers between devices  41.4 us (17%)
  matrix products  34.7 us (15%)
  starting transfers between devices  7.51 us (3%)
    all_to_all x1, blocking collectives, shards(): lax.all_to_all(outgoing_back, 'shots', split_axis=2, concat_axis=0, tiled...  58.5 us
    convert_element_type x1, local copies, waits for them, and re-layouts, shards(): multiples.astype(jnp.bfloat16)  44.2 us
    all_to_all x1, waiting for transfers between devices, lay_group_up(): lax.all_to_all(jnp.stack(jnp.split(z, lax.psum(1, peer_axis), 0)), peer_a...  41.4 us
    unnamed x32, local copies, waits for them, and re-layouts  14.2 us
    dot_general x1, matrix products, shards(): jnp.einsum('shrt,tpc->phcsr', blocked, forward, preferred_element_type=jn...  14.2 us
    dot_general x1, matrix products, shards(): jnp.einsum('phsir,pit->shrt', returned, inverse_pair, preferred_element_t...  14.1 us
    gather x3, local copies, waits for them, and re-layouts, shards(): picked = jnp.take(own_block, neighbours[:, slot_index], axis=2)  8.18 us
    reshape x3, local copies, waits for them, and re-layouts, lay_group_up(): jnp.concatenate(lax.all_to_all(jnp.stack(jnp.split(z, lax.psum(1, peer_ax...  7.59 us
  transfers between devices with their start and end apart: 2, of which 1 were waited for; matrix products, arithmetic and copies ran while one was open for 3% of the time, Pallas kernels for 0%

profile of v1, /device:TPU:1, one launch (start us, length us, event | category | flops | bytes accessed | tf_op | source)
XLA Modules:
  0.0 235.5 jit_solution(17644771592506310387)
XLA Ops:
  0.0 0.8 fusion.49
  0.8 14.2 %convert_bitcast_fusion = bf16[8,2,2,64,512]{4,0,1,3,2:T(8,128)(2,1)S(1)} fusion(bf16[64,2,512,256,1]{3,2,1,0,4:T(8,128)(2,1)} %bitcast.189, f32[256,8,1]{0,1,2:T(8,128)S(1)} %get-tuple-element.30, f32[256,8,1]{0,1,2:T(8,128)S(1)} %get-tuple-element.29), kind=kOutput, calls=%fused_computation.31 | convolution fusion | flops 537931776 | bytes 35667968 | tf_op jit(solution)/shard_map/shrt,tpc->phcsr/dot_general | solution.py:61
  15.0 1.2 copy.55
  16.1 0.7 fusion.36
  18.8 0.7 fusion.32
  20.1 0.7 fusion.30
  26.8 7.4 %all-to-all-start = ((bf16[16,1,2,64,512]{4,3,2,1,0:T(8,128)(2,1)}), bf16[16,1,2,64,512]{4,3,2,1,0:T(8,128)(2,1)S(1)}, u32[]{:S(2)}, u32[]{:S(2)}) async-start(bf16[16,1,2,64,512]{4,3,2,1,0:T(8,128)(2,1)} %fusion.21), calls=%async_computation | async-start | bytes 4194304 | tf_op jit(solution)/shard_map/all_to_all | solution.py:11
  34.3 41.4 %all-to-all-done = bf16[16,1,2,64,512]{4,3,2,1,0:T(8,128)(2,1)S(1)} async-done(((bf16[16,1,2,64,512]{4,3,2,1,0:T(8,128)(2,1)}), bf16[16,1,2,64,512]{4,3,2,1,0:T(8,128)(2,1)S(1)}, u32[]{:S(2)}, u32[]{:S(2)}) %all-to-all-start) | async-done | bytes 2097184 | tf_op jit(solution)/shard_map/all_to_all | solution.py:11
  75.8 1.3 copy-done
  77.1 3.9 %copy.56 = bf16[1,2,16,64,512]{4,1,3,2,0:T(2,128)(2,1)S(1)} copy(bf16[1,2,16,64,512]{4,3,1,0,2:T(8,128)(2,1)} %bitcast.190) | data formatting | bytes 4194304 | tf_op jit(solution)/shard_map/reshape | solution.py:10
  81.2 3.5 %copy.92 = bf16[1,2,1024,512]{3,1,2,0:T(2,128)(2,1)} copy(bf16[1,2,1024,512]{3,2,1,0:T(8,128)(2,1)S(1)} %bitcast.209) | data formatting | bytes 4194304 | tf_op jit(solution)/shard_map/reshape | solution.py:10
  84.7 2.7 %gather_fusion.2 = bf16[128,2,512]{2,1,0:T(2,128)(2,1)S(1)} fusion(bf16[2,1024,512]{2,0,1:T(2,128)(2,1)} %bitcast.214, s32[1024]{0:T(1024)S(1)} %get-tuple-element.31), kind=kCustom, calls=%fused_computation.2.clone | custom fusion | bytes 524800 | tf_op jit(solution)/shard_map/jit(_take)/gather | solution.py:71
  87.4 2.7 %gather_fusion.1 = bf16[128,2,512]{2,1,0:T(2,128)(2,1)S(1)} fusion(bf16[2,1024,512]{2,0,1:T(2,128)(2,1)} %bitcast.215, s32[1024]{0:T(1024)S(1)} %get-tuple-element.32), kind=kCustom, calls=%fused_computation.1.clone | custom fusion | bytes 524800 | tf_op jit(solution)/shard_map/jit(_take)/gather | solution.py:71
  90.2 2.7 %gather_fusion = bf16[128,2,512]{2,1,0:T(2,128)(2,1)S(1)} fusion(bf16[2,1024,512]{2,0,1:T(2,128)(2,1)} %bitcast.216, s32[1024]{0:T(1024)S(1)} %pad_clamp_fusion.2), kind=kCustom, calls=%fused_computation.clone | custom fusion | bytes 524800 | tf_op jit(solution)/shard_map/jit(_take)/gather | solution.py:71
  93.5 4.4 %scatter_fusion = bf16[2,1024,512]{2,0,1:T(2,128)(2,1)S(1)} fusion(bf16[2,1024,512]{2,0,1:T(2,128)(2,1)S(1)} %bitcast.186, s32[128]{0:T(128)S(1)} %compare_select_fusion.3, bf16[128,2,512]{2,1,0:T(2,128)(2,1)S(1)} %copy.64), kind=kCustom, calls=%fused_computation.3 | custom fusion | bytes 786944 | tf_op jit(solution)/shard_map/scatter | solution.py:73
  97.8 1.4 constant_dynamic-slice_fusion
  99.7 3.2 %fusion.59 = (bf16[1,1,1024,512]{3,1,2,0:T(2,128)(2,1)S(1)}, bf16[1,1,1024,512]{3,1,2,0:T(2,128)(2,1)S(1)}) fusion(bf16[1,2,1024,512]{3,1,2,0:T(2,128)(2,1)S(1)} %bitcast.188), kind=kLoop, calls=%fused_computation.121 | loop fusion | bytes 4194304 | tf_op jit(solution)/shard_map/slice | solution.py:37
  103.8 2.5 %fusion.1 = f32[1024,1024]{0,1:T(8,128)S(1)} fusion(bf16[1,1024,512]{2,1,0:T(8,128)(2,1)S(1)} %bitcast.219, bf16[1,1024,512]{2,1,0:T(8,128)(2,1)S(1)} %bitcast.218, bf16[1,512,512]{2,1,0:T(8,128)(2,1)S(1)} %get-tuple-element.21, bf16[1,512,512]{2,1,0:T(8,128)(2,1)S(1)} %fusion.56, bf16[1,512,512]{2,1,0:T(8,128)(2,1)S(1)} %get-tuple-element.20), kind=kOutput, calls=%fused_computation.8 | convolution fusion | flops 2160066560 | bytes 7864320 | tf_op jit(solution)/shard_map/zsk,zkc->zsc/dot_general | solution.py:45
  106.2 3.0 %fusion.58 = (bf16[1,1,1024,512]{3,1,2,0:T(2,128)(2,1)S(1)}, bf16[1,1,1024,512]{3,1,2,0:T(2,128)(2,1)S(1)}) fusion(bf16[1,2,1024,512]{3,1,2,0:T(2,128)(2,1)S(1)} %collective-permute-done), kind=kLoop, calls=%fused_computation.120 | loop fusion | bytes 4194304 | tf_op jit(solution)/shard_map/slice | solution.py:37
  109.8 4.0 %multiply_convert_fusion = bf16[1024,1024]{0,1:T(8,128)(2,1)} fusion(f32[1024,1024]{0,1:T(8,128)S(1)} %fusion.1, bf16[1,512,512]{2,1,0:T(8,128)(2,1)S(1)} %get-tuple-element.19, bf16[1,512,512]{2,1,0:T(8,128)(2,1)S(1)} %fusion.57, bf16[1,512,512]{2,1,0:T(8,128)(2,1)S(1)} %get-tuple-element.18, bf16[1,1024,512]{2,1,0:T(8,128)(2,1)S(1)} %bitcast.221, ...), kind=kOutput, calls=%fused_computation.6 | convolution fusion | flops 2163212288 | bytes 9961472 | tf_op jit(solution)/shard_map/zsk,zkc->zsc/dot_general | solution.py:45
  113.8 4.8 %copy.67 = bf16[1,1,1024,2,512]{4,3,1,0,2:T(2,128)(2,1)S(1)} copy(bf16[1,1,1024,2,512]{2,4,3,1,0:T(8,128)(2,1)} %bitcast.217) | data formatting | bytes 4194304 | tf_op jit(solution)/shard_map/reshape | solution.py:81
  118.6 58.5 %all_to_all.14 = bf16[1,1,1024,2,512]{4,3,1,0,2:T(2,128)(2,1)S(1)} all-to-all(bf16[1,1,1024,2,512]{4,3,1,0,2:T(2,128)(2,1)S(1)} %copy.67), channel_id=1, replica_groups=mesh['lines'=2,'shots'=16] {'shots'}, dimensions={2} | all-to-all | bytes 4194304 | tf_op jit(solution)/shard_map/all_to_all | solution.py:82
  177.1 14.1 %fusion = bf16[64,2,512,256]{2,3,0,1:T(8,128)(2,1)} fusion(bf16[8,2,64,2,512]{4,3,2,1,0:T(2,128)(2,1)S(1)} %bitcast.192, f32[256,8,1]{0,1,2:T(8,128)S(1)} %get-tuple-element.30, f32[256,8,1]{0,1,2:T(8,128)S(1)} %get-tuple-element.29), kind=kOutput, calls=%fused_computation.5 | convolution fusion | flops 553660416 | bytes 35667968 | tf_op jit(solution)/shard_map/phsir,pit->shrt/dot_general | solution.py:85
  191.3 44.2 %copy.70 = bf16[64,2,512,256]{3,2,1,0:T(8,128)(2,1)} copy(bf16[64,2,512,256]{2,3,0,1:T(8,128)(2,1)} %fusion) | data formatting | bytes 67108864 | tf_op jit(solution)/shard_map/convert_element_type | solution.py:88
  (42 shorter events, 11.2 us)
Async XLA Ops:
  26.8 7.5 %copy-start.3 = (s32[128,3]{0,1:T(4,128)S(1)}, s32[128,3]{0,1:T(4,128)}, u32[]{:S(2)}) copy-start(s32[128,3]{0,1:T(4,128)} %param.9) | copy-start | bytes 4612
  26.8 7.5 %copy-start.4 = (s32[128]{0:T(128)S(1)}, s32[128]{0:T(128)}, u32[]{:S(2)}) copy-start(s32[128]{0:T(128)} %param.8) | copy-start | bytes 1540
  26.8 7.5 %copy-start.2 = (f32[128,3]{0,1:T(4,128)S(1)}, f32[128,3]{0,1:T(4,128)}, u32[]{:S(2)}) copy-start(f32[128,3]{0,1:T(4,128)} %param.10) | copy-start | bytes 4612
  26.8 49.0 %all-to-all-start = ((bf16[16,1,2,64,512]{4,3,2,1,0:T(8,128)(2,1)}), bf16[16,1,2,64,512]{4,3,2,1,0:T(8,128)(2,1)S(1)}, u32[]{:S(2)}, u32[]{:S(2)}) async-start(bf16[16,1,2,64,512]{4,3,2,1,0:T(8,128)(2,1)} %fusion.21), calls=%async_computation | async-start | bytes 4194304 | tf_op jit(solution)/shard_map/all_to_all | solution.py:11
  75.8 1.3 copy-start
  77.1 3.9 %copy-start.1 = (bf16[16,1,2,64,512]{4,3,2,1,0:T(8,128)(2,1)S(1)}, bf16[16,1,2,64,512]{4,3,2,1,0:T(8,128)(2,1)}, u32[]{:S(2)}) copy-start(bf16[16,1,2,64,512]{4,3,2,1,0:T(8,128)(2,1)} %copy-done) | copy-start | bytes 6291460
  99.6 6.6 %collective-permute-start = (bf16[1,2,1024,512]{3,1,2,0:T(2,128)(2,1)S(1)}, bf16[1,2,1024,512]{3,1,2,0:T(2,128)(2,1)S(1)}, u32[]{:S(2)}, u32[]{:S(2)}) collective-permute-start(bf16[1,2,1024,512]{3,1,2,0:T(2,128)(2,1)S(1)} %bitcast.187), channel_id=1, source_target_pairs={{0,1},{1,0},{2,3},{3,2},{4,5},{5,4},{6,7},{7,6},{8,9},{9,8},{10,11... | collective-permute-start | bytes 6291464 | tf_op jit(solution)/shard_map/ppermute | solution.py:19
